TPU v7x, 32 devices: a whole 2x2x4 slice. The times are simulated.
32 devices in a mesh: src: 8 (over z, y), space: 4 (over x, core).
Axes of the slice: x: 2, y: 2, z: 4, core: 2. Of those that a mesh axis runs over, the one named last changes fastest.
Arguments:
- wavefield: float32 [8, 9, 32, 64, 128], P('src', None, 'space'), may hold values from -6 to 6
- strain_bank: bfloat16 [8, 6, 32, 64, 128], P('src', None, 'space'), may hold values from -6 to 6
- owners: int32 [4], replicated, may hold values from 0 to 7, as said below
- region: int32 [32, 64, 128], P('space'), may hold values from 0 to 7
- region_lambda: float32 [8], replicated, may hold values from 1 to 2
- region_mu: float32 [8], replicated, may hold values from 0.5 to 1
- region_buoyancy: float32 [8], replicated, may hold values from 0.5 to 1
Outputs:
- new_wavefield: float32 [8, 9, 32, 64, 128], P('src', None, 'space')
- lambda_kernel: float32 [32, 64, 128], P('space', 'src')
- mu_kernel: float32 [32, 64, 128], P('space', 'src')
Inputs may be any that keep to these rules, and one draw needn't show every extreme that they name: `owners`: 4 distinct owner indices in an order drawn per run; 0 and 7 are always among them.
All inputs are finite; a program needn't handle non-finite values.
Results may differ from a plain program's by a relative error of at most 0.0003.
Values may be sent and summed in bfloat16 or wider, within the bound.
A program may use at most 128 MiB of HBM per device.

v0:
```python
import jax
import jax.numpy as jnp
from jax import lax
from jax.sharding import PartitionSpec as P

STEPS = 4


step_size = 0.3
x_force_terms = (0, 5, 4)
y_force_terms = (5, 1, 3)
z_force_terms = (4, 3, 2)


def spread(block, axis, owner):
    block = jnp.where(lax.axis_index(axis) == owner, block, jnp.zeros_like(block))
    return lax.psum(block, axis)


def extended(x, sides, width):
    for axis, dim in sides:
        devices, length = (lax.axis_size(axis), x.shape[dim])
        up = [(i, (i + 1) % devices) for i in range(devices - 1)]
        down = [(j, i) for i, j in up]
        last = lax.slice_in_dim(x, length - width, length, axis=dim)
        initial = lax.slice_in_dim(x, 0, width, axis=dim)
        before = lax.ppermute(last, axis, up)
        after = lax.ppermute(initial, axis, down)
        x = jnp.concatenate([before, x, after], axis=dim)
    return x


def slab_of(values, along, start, length):
    slicer = [slice(None)] * values.ndim
    slicer[values.ndim + along] = slice(start, start + length)
    return values[tuple(slicer)]


def diff_valid(padded, along):
    length = padded.shape[along] - 4
    near = slab_of(padded, along, 3, length) - slab_of(padded, along, 1, length)
    far = slab_of(padded, along, 4, length) - slab_of(padded, along, 0, length)
    return (8.0 * near - far) / 12.0


def diff_zero(values, along):
    widths = [(0, 0)] * values.ndim
    widths[values.ndim + along] = (2, 2)
    return diff_valid(jnp.pad(values, widths), along)


def component(values, which):
    return values[..., which, :, :, :]


def pick_terms(values, order):
    return jnp.stack([component(values, which) for which in order], -4)


def stress_update(stress, grad_x, grad_y, grad_z, lame_first, shear):
    diagonal = [component(grad_x, 0), component(grad_y, 1), component(grad_z, 2)]
    divergence = diagonal[0] + diagonal[1] + diagonal[2]
    parts = [
        component(stress, which)
        + step_size * (lame_first * divergence + 2.0 * shear * diagonal[which])
        for which in range(3)
    ]
    parts.append(
        component(stress, 3) + step_size * shear * (component(grad_z, 1) + component(grad_y, 2))
    )
    parts.append(
        component(stress, 4) + step_size * shear * (component(grad_z, 0) + component(grad_x, 2))
    )
    parts.append(
        component(stress, 5) + step_size * shear * (component(grad_y, 0) + component(grad_x, 1))
    )
    return jnp.stack(parts, -4)


def correlate(stress, receiver, lame_first, shear):
    trace = component(stress, 0) + component(stress, 1) + component(stress, 2)
    theta = trace / (3.0 * lame_first + 2.0 * shear)
    recv_trace = receiver[0] + receiver[1] + receiver[2]
    term_lambda = step_size * theta * recv_trace
    inner = jnp.zeros_like(theta)
    for which in range(3):
        inner = (
            inner
            + (component(stress, which) - lame_first * theta) / (2.0 * shear) * receiver[which]
        )
    for which in range(3, 6):
        inner = inner + component(stress, which) / shear * receiver[which]
    term_mu = step_size * 2.0 * inner
    return (term_lambda, term_mu)


def material(region, region_lambda, region_mu, region_buoyancy):
    labels = jnp.arange(region_lambda.shape[0], dtype=jnp.int32)
    onehot = (region[None] == labels[:, None, None, None]).astype(jnp.float32)
    return [
        jnp.sum(onehot * table[:, None, None, None], 0)
        for table in (region_lambda, region_mu, region_buoyancy)
    ]


def local(wavefield, strain_bank, owners, region, region_lambda, region_mu, region_buoyancy):
    lame_first, shear, buoyancy = material(region, region_lambda, region_mu, region_buoyancy)
    state = wavefield
    kernel_lambda = jnp.zeros(region.shape, jnp.float32)
    kernel_mu = jnp.zeros(region.shape, jnp.float32)
    for time_step in range(STEPS):
        receiver = spread(strain_bank, "src", owners[time_step])[0].astype(jnp.float32)
        velocity = state[:, 0:3]
        stress = state[:, 3:9]
        padded = extended(stress, (("space", 2),), 2)
        force = (
            diff_valid(pick_terms(padded, x_force_terms), -3)
            + diff_zero(pick_terms(stress, y_force_terms), -2)
            + diff_zero(pick_terms(stress, z_force_terms), -1)
        )
        velocity = velocity + step_size * buoyancy * force
        grad_x = diff_valid(extended(velocity, (("space", 2),), 2), -3)
        stress = stress_update(
            stress, grad_x, diff_zero(velocity, -2), diff_zero(velocity, -1), lame_first, shear
        )
        state = jnp.concatenate([velocity, stress], -4)
        term_lambda, term_mu = correlate(stress, receiver, lame_first, shear)
        kernel_lambda = kernel_lambda + jnp.sum(term_lambda, 0)
        kernel_mu = kernel_mu + jnp.sum(term_mu, 0)
    summed = (
        lax.psum_scatter(kernel_lambda, "src", scatter_dimension=1, tiled=True),
        lax.psum_scatter(kernel_mu, "src", scatter_dimension=1, tiled=True),
    )
    return (state, summed[0], summed[1])


def solution(mesh):
    in_specs = (
        P("src", None, "space", None, None),
        P("src", None, "space", None, None),
        P(),
        P("space", None, None),
        P(),
        P(),
        P(),
    )
    out_specs = (
        P("src", None, "space", None, None),
        P("space", "src", None),
        P("space", "src", None),
    )
    return jax.shard_map(local, mesh=mesh, in_specs=in_specs, out_specs=out_specs, check_vma=False)
```

profile of v0, /device:TPU:0, one launch (start us, length us, event | category | flops | bytes accessed | tf_op | source)
XLA Modules:
  0.0 368.2 jit_solution(11685846996095671835)
XLA Ops:
  7.2 1.2 fusion.273
  8.4 2.6 collective-permute-start
  11.0 1.3 collective-permute-start.1
  12.3 1.4 fusion.274
  14.9 1.8 collective-permute-done.1
  17.6 1.3 collective-permute-start.2
  18.9 8.5 %collective-permute-start.3 = (f32[1,3,2,64,128]{4,3,2,1,0:T(8,128)S(1)}, f32[1,3,2,64,128]{4,3,2,1,0:T(8,128)S(1)}, u32[]{:S(2)}, u32[]{:S(2)}) collective-permute-start(f32[1,3,2,64,128]{4,3,2,1,0:T(8,128)S(1)} %get-tuple-element.87), channel_id=1, source_target_pairs={{0,1},{1,2},{2,3},{4,5},{5,6},{6,7},{8,9},{9,10},{10,11},{12,13},{... | collective-permute-start | bytes 589832 | tf_op jit(solution)/shard_map/ppermute | solution.py:27
  27.4 1.0 collective-permute-done.3
  28.4 1.3 fusion.14
  31.4 5.2 %collective-permute-start.4 = (f32[1,6,2,64,128]{4,3,2,1,0:T(8,128)S(1)}, f32[1,6,2,64,128]{4,3,2,1,0:T(8,128)S(1)}, u32[]{:S(2)}, u32[]{:S(2)}) collective-permute-start(f32[1,6,2,64,128]{4,3,2,1,0:T(8,128)S(1)} %get-tuple-element.62), channel_id=1, source_target_pairs={{0,1},{1,2},{2,3},{4,5},{5,6},{6,7},{8,9},{9,10},{10,11},{12,13},{... | collective-permute-start | bytes 1179656 | tf_op jit(solution)/shard_map/ppermute | solution.py:27
  36.6 1.3 collective-permute-start.5
  38.5 3.7 collective-permute-done.5
  43.8 1.3 collective-permute-start.6
  45.1 9.2 %collective-permute-start.7 = (f32[1,3,2,64,128]{4,3,2,1,0:T(8,128)}, f32[1,3,2,64,128]{4,3,2,1,0:T(8,128)}, u32[]{:S(2)}, u32[]{:S(2)}) collective-permute-start(f32[1,3,2,64,128]{4,3,2,1,0:T(8,128)} %get-tuple-element.82), channel_id=1, source_target_pairs={{0,1},{1,2},{2,3},{4,5},{5,6},{6,7},{8,9},{9,10},{10,11},{12,13},{... | collective-permute-start | bytes 589832 | tf_op jit(solution)/shard_map/ppermute | solution.py:27
  55.0 6.4 %fusion.19 = (f32[1,3,8,64,128]{4,3,2,1,0:T(8,128)S(1)}, f32[1,3,8,64,128]{4,3,2,1,0:T(8,128)S(1)}, f32[1,3,8,64,128]{4,3,2,1,0:T(8,128)S(1)}) fusion(f32[1,3,8,64,128]{4,3,2,1,0:T(8,128)} %copy-done.18, f32[1,3,2,64,128]{4,3,2,1,0:T(8,128)} %collective-permute-done.7, f32[1,3,2,64,128]{4,3,2,1,0:T(8,128)} %collective-permute-done.6), kind=kLoop, calls=%fused_computation.119 | loop fusion | flops 3735552 | bytes 3538944 | tf_op jit(solution)/shard_map/div | solution.py:43
  61.5 2.2 constant_dynamic-update-slice_fusion.11
  67.1 1.1 copy-done.23
  68.2 0.9 fusion.276
  69.1 5.9 %collective-permute-start.8 = (f32[1,6,2,64,128]{4,3,2,1,0:T(8,128)}, f32[1,6,2,64,128]{4,3,2,1,0:T(8,128)}, u32[]{:S(2)}, u32[]{:S(2)}) collective-permute-start(f32[1,6,2,64,128]{4,3,2,1,0:T(8,128)} %get-tuple-element.60), channel_id=1, source_target_pairs={{0,1},{1,2},{2,3},{4,5},{5,6},{6,7},{8,9},{9,10},{10,11},{12,13},{... | collective-permute-start | bytes 1179656 | tf_op jit(solution)/shard_map/ppermute | solution.py:27
  75.0 1.3 collective-permute-start.9
  79.5 1.2 select_maximum_fusion.34
  81.2 0.9 copy-done.24
  82.1 1.4 fusion.3
  85.0 1.3 collective-permute-start.10
  86.3 7.3 %collective-permute-start.11 = (f32[1,3,2,64,128]{4,3,2,1,0:T(8,128)}, f32[1,3,2,64,128]{4,3,2,1,0:T(8,128)}, u32[]{:S(2)}, u32[]{:S(2)}) collective-permute-start(f32[1,3,2,64,128]{4,3,2,1,0:T(8,128)} %get-tuple-element.77), channel_id=1, source_target_pairs={{0,1},{1,2},{2,3},{4,5},{5,6},{6,7},{8,9},{9,10},{10,11},{12,13},{... | collective-permute-start | bytes 589832 | tf_op jit(solution)/shard_map/ppermute | solution.py:27
  93.7 1.7 broadcast_select_fusion
  95.7 6.3 %fusion.24 = (f32[1,3,8,64,128]{4,3,2,1,0:T(8,128)S(1)}, f32[1,3,8,64,128]{4,3,2,1,0:T(8,128)S(1)}, f32[1,3,8,64,128]{4,3,2,1,0:T(8,128)S(1)}) fusion(f32[1,3,8,64,128]{4,3,2,1,0:T(8,128)} %copy-done.16, f32[1,3,2,64,128]{4,3,2,1,0:T(8,128)} %collective-permute-done.11, f32[1,3,2,64,128]{4,3,2,1,0:T(8,128)} %collective-permute-done.10), kind=kLoop, calls=%fused_computation.124 | loop fusion | flops 3735552 | bytes 3538944 | tf_op jit(solution)/shard_map/div | solution.py:43
  102.2 1.0 copy-done.33
  105.3 3.9 %collective-permute-start.12 = (f32[1,6,2,64,128]{4,3,2,1,0:T(8,128)S(1)}, f32[1,6,2,64,128]{4,3,2,1,0:T(8,128)S(1)}, u32[]{:S(2)}, u32[]{:S(2)}) collective-permute-start(f32[1,6,2,64,128]{4,3,2,1,0:T(8,128)S(1)} %get-tuple-element.58), channel_id=1, source_target_pairs={{0,1},{1,2},{2,3},{4,5},{5,6},{6,7},{8,9},{9,10},{10,11},{12,13},{... | collective-permute-start | bytes 1179656 | tf_op jit(solution)/shard_map/ppermute | solution.py:27
  109.2 1.3 collective-permute-start.13
  111.1 3.7 collective-permute-done.13
  114.9 1.6 constant_dynamic-update-slice_fusion.18
  116.5 1.3 collective-permute-start.14
  117.8 9.1 %collective-permute-start.15 = (f32[1,3,2,64,128]{4,3,2,1,0:T(8,128)S(1)}, f32[1,3,2,64,128]{4,3,2,1,0:T(8,128)S(1)}, u32[]{:S(2)}, u32[]{:S(2)}) collective-permute-start(f32[1,3,2,64,128]{4,3,2,1,0:T(8,128)S(1)} %get-tuple-element.72), channel_id=1, source_target_pairs={{0,1},{1,2},{2,3},{4,5},{5,6},{6,7},{8,9},{9,10},{10,11},{12,13},{... | collective-permute-start | bytes 589832 | tf_op jit(solution)/shard_map/ppermute | solution.py:27
  126.9 1.0 collective-permute-done.15
  127.9 1.3 fusion.29
  129.2 1.1 fusion.247
  131.9 93.7 %all-reduce.19.cloned.1.call-done = (bf16[1,6,8,64,128]{4,3,2,1,0:T(8,128)(2,1)}, bf16[1,6,8,64,128]{4,3,2,1,0:T(8,128)(2,1)}, bf16[1,6,8,64,128]{4,3,2,1,0:T(8,128)(2,1)}, bf16[1,6,8,64,128]{4,3,2,1,0:T(8,128)(2,1)}) async-done(((bf16[1,6,8,64,128]{4,3,2,1,0:T(8,128)(2,1)}, bf16[1,6,8,64,128]{4,3,2,1,0:T(8,128)(2,1)}, bf16[1,6,8,64,128]{4,3,2,1,0:T(8,128)(2,1)}, bf16[1,6,8,64,128]{4,3,2,1,0:T(8,128)(2,1)}), ...) | async-done | bytes 3145744 | tf_op jit(solution)/shard_map/psum | solution.py:17
  225.5 1.4 convert_element_type.35
  227.1 1.5 copy-done.51
  230.0 1.1 copy-done.15
  231.1 3.5 add_bitcast_fusion
  234.7 7.4 %fusion.123 = f32[8,64,128]{2,1,0:T(8,128)} fusion(f32[1,6,8,64,128]{4,3,2,1,0:T(8,128)} %copy-done.15, f32[1,6,8,64,128]{4,3,2,1,0:T(8,128)} %copy-done.14, f32[1,6,8,64,128]{4,3,2,1,0:T(8,128)} %copy-done.13, f32[1,6,8,64,128]{4,3,2,1,0:T(8,128)} %copy-done.12, f32[8,64,128]{2,1,0:T(8,128)S(1)} %get-tuple-element.3, ...), kind=kLoop, calls=%fused_computation.260 | loop fusion | flops 13107200 | bytes 18087936 | tf_op jit(solution)/shard_map/add | solution.py:129
  242.2 1.9 fusion.212
  244.1 1.7 fusion.214
  245.8 1.7 fusion.216
  247.5 48.8 %reduce-scatter.3.cloned.1.call-done = f32[8,8,128]{2,1,0:T(8,128)} async-done(((f32[8,64,128]{2,1,0:T(8,128)}), f32[8,8,128]{2,1,0:T(8,128)}) %reduce-scatter.3.cloned.1.call-update) | async-done | bytes 32784 | tf_op jit(solution)/shard_map/reduce_scatter | solution.py:131
  296.3 65.4 %reduce-scatter.5.cloned.1.call-done = f32[8,8,128]{2,1,0:T(8,128)} async-done(((f32[8,64,128]{2,1,0:T(8,128)}), f32[8,8,128]{2,1,0:T(8,128)}) %reduce-scatter.5.cloned.1.call-update) | async-done | bytes 32784 | tf_op jit(solution)/shard_map/reduce_scatter | solution.py:132
  (174 shorter events, 18.8 us)
Async XLA Ops:
  7.2 218.4 %all-reduce.19.cloned.1.call-start = ((), (), s32[]{:S(2)}) async-start(), calls=%async_computation.4 | async-start | bytes 6291456 | tf_op jit(solution)/shard_map/psum | solution.py:17
  8.4 5.3 %copy-start.53 = (s32[8,64,128]{2,1,0:T(8,128)S(1)}, s32[8,64,128]{2,1,0:T(8,128)}, u32[]{:S(2)}) copy-start(s32[8,64,128]{2,1,0:T(8,128)} %param.10) | copy-start | bytes 786436
  8.4 5.3 %copy-start.55 = (f32[8]{0:T(128)S(1)}, f32[8]{0:T(128)}, u32[]{:S(2)}) copy-start(f32[8]{0:T(128)} %param.12) | copy-start | bytes 100
  8.4 5.3 %copy-start.56 = (f32[8]{0:T(128)S(1)}, f32[8]{0:T(128)}, u32[]{:S(2)}) copy-start(f32[8]{0:T(128)} %param.11) | copy-start | bytes 100
  8.4 5.3 %copy-start.57 = (f32[8]{0:T(128)S(1)}, f32[8]{0:T(128)}, u32[]{:S(2)}) copy-start(f32[8]{0:T(128)} %param.13) | copy-start | bytes 100
  8.4 6.4 %collective-permute-start = (f32[1,6,2,64,128]{4,3,2,1,0:T(8,128)S(1)}, f32[1,6,2,64,128]{4,3,2,1,0:T(8,128)S(1)}, u32[]{:S(2)}, u32[]{:S(2)}) collective-permute-start(f32[1,6,2,64,128]{4,3,2,1,0:T(8,128)S(1)} %get-tuple-element.51), channel_id=1, source_target_pairs={{0,1},{1,2},{2,3},{4,5},{5,6},{6,7},{8,9},{9,10},{10,11},{12,13},{... | collective-permute-start | bytes 1179656 | tf_op jit(solution)/shard_map/ppermute | solution.py:27
  11.0 5.7 %collective-permute-start.1 = (f32[1,6,2,64,128]{4,3,2,1,0:T(8,128)S(1)}, f32[1,6,2,64,128]{4,3,2,1,0:T(8,128)S(1)}, u32[]{:S(2)}, u32[]{:S(2)}) collective-permute-start(f32[1,6,2,64,128]{4,3,2,1,0:T(8,128)S(1)} %get-tuple-element.52), channel_id=1, source_target_pairs={{1,0},{2,1},{3,2},{5,4},{6,5},{7,6},{9,8},{10,9},{11,10},{13,12},{... | collective-permute-start | bytes 1179656 | tf_op jit(solution)/shard_map/ppermute | solution.py:28
  17.6 9.8 %collective-permute-start.2 = (f32[1,3,2,64,128]{4,3,2,1,0:T(8,128)S(1)}, f32[1,3,2,64,128]{4,3,2,1,0:T(8,128)S(1)}, u32[]{:S(2)}, u32[]{:S(2)}) collective-permute-start(f32[1,3,2,64,128]{4,3,2,1,0:T(8,128)S(1)} %get-tuple-element.86), channel_id=1, source_target_pairs={{1,0},{2,1},{3,2},{5,4},{6,5},{7,6},{9,8},{10,9},{11,10},{13,12},{... | collective-permute-start | bytes 589832 | tf_op jit(solution)/shard_map/ppermute | solution.py:28
  18.9 9.6 %collective-permute-start.3 = (f32[1,3,2,64,128]{4,3,2,1,0:T(8,128)S(1)}, f32[1,3,2,64,128]{4,3,2,1,0:T(8,128)S(1)}, u32[]{:S(2)}, u32[]{:S(2)}) collective-permute-start(f32[1,3,2,64,128]{4,3,2,1,0:T(8,128)S(1)} %get-tuple-element.87), channel_id=1, source_target_pairs={{0,1},{1,2},{2,3},{4,5},{5,6},{6,7},{8,9},{9,10},{10,11},{12,13},{... | collective-permute-start | bytes 589832 | tf_op jit(solution)/shard_map/ppermute | solution.py:27
  30.0 7.9 %copy-start.45 = (f32[1,1,8,64,128]{4,3,2,1,0:T(8,128)}, f32[1,1,8,64,128]{4,3,2,1,0:T(8,128)S(1)}, u32[]{:S(2)}) copy-start(f32[1,1,8,64,128]{4,3,2,1,0:T(8,128)S(1)} %get-tuple-element.48) | copy-start | bytes 786436
  30.1 7.9 %copy-start.43 = (f32[1,1,8,64,128]{4,3,2,1,0:T(8,128)}, f32[1,1,8,64,128]{4,3,2,1,0:T(8,128)S(1)}, u32[]{:S(2)}) copy-start(f32[1,1,8,64,128]{4,3,2,1,0:T(8,128)S(1)} %get-tuple-element.46) | copy-start | bytes 786436
  30.2 7.8 %copy-start.27 = (f32[1,1,8,64,128]{4,3,2,1,0:T(8,128)}, f32[1,1,8,64,128]{4,3,2,1,0:T(8,128)S(1)}, u32[]{:S(2)}) copy-start(f32[1,1,8,64,128]{4,3,2,1,0:T(8,128)S(1)} %get-tuple-element.44) | copy-start | bytes 786436
  30.7 7.3 %copy-start.41 = (f32[1,1,8,64,128]{4,3,2,1,0:T(8,128)}, f32[1,1,8,64,128]{4,3,2,1,0:T(8,128)S(1)}, u32[]{:S(2)}) copy-start(f32[1,1,8,64,128]{4,3,2,1,0:T(8,128)S(1)} %get-tuple-element.42) | copy-start | bytes 786436
  31.3 6.7 %copy-start.39 = (f32[1,1,8,64,128]{4,3,2,1,0:T(8,128)}, f32[1,1,8,64,128]{4,3,2,1,0:T(8,128)S(1)}, u32[]{:S(2)}) copy-start(f32[1,1,8,64,128]{4,3,2,1,0:T(8,128)S(1)} %get-tuple-element.40) | copy-start | bytes 786436
  31.4 7.1 %collective-permute-start.4 = (f32[1,6,2,64,128]{4,3,2,1,0:T(8,128)S(1)}, f32[1,6,2,64,128]{4,3,2,1,0:T(8,128)S(1)}, u32[]{:S(2)}, u32[]{:S(2)}) collective-permute-start(f32[1,6,2,64,128]{4,3,2,1,0:T(8,128)S(1)} %get-tuple-element.62), channel_id=1, source_target_pairs={{0,1},{1,2},{2,3},{4,5},{5,6},{6,7},{8,9},{9,10},{10,11},{12,13},{... | collective-permute-start | bytes 1179656 | tf_op jit(solution)/shard_map/ppermute | solution.py:27
  36.6 5.6 %collective-permute-start.5 = (f32[1,6,2,64,128]{4,3,2,1,0:T(8,128)S(1)}, f32[1,6,2,64,128]{4,3,2,1,0:T(8,128)S(1)}, u32[]{:S(2)}, u32[]{:S(2)}) collective-permute-start(f32[1,6,2,64,128]{4,3,2,1,0:T(8,128)S(1)} %get-tuple-element.63), channel_id=1, source_target_pairs={{1,0},{2,1},{3,2},{5,4},{6,5},{7,6},{9,8},{10,9},{11,10},{13,12},{... | collective-permute-start | bytes 1179656 | tf_op jit(solution)/shard_map/ppermute | solution.py:28
  43.0 11.3 %copy-start.18 = (f32[1,3,8,64,128]{4,3,2,1,0:T(8,128)}, f32[1,3,8,64,128]{4,3,2,1,0:T(8,128)S(1)}, u32[]{:S(2)}) copy-start(f32[1,3,8,64,128]{4,3,2,1,0:T(8,128)S(1)} %fusion.101) | copy-start | bytes 2359300
  43.8 10.5 %collective-permute-start.6 = (f32[1,3,2,64,128]{4,3,2,1,0:T(8,128)}, f32[1,3,2,64,128]{4,3,2,1,0:T(8,128)}, u32[]{:S(2)}, u32[]{:S(2)}) collective-permute-start(f32[1,3,2,64,128]{4,3,2,1,0:T(8,128)} %get-tuple-element.81), channel_id=1, source_target_pairs={{1,0},{2,1},{3,2},{5,4},{6,5},{7,6},{9,8},{10,9},{11,10},{13,12},{... | collective-permute-start | bytes 589832 | tf_op jit(solution)/shard_map/ppermute | solution.py:28
  45.1 9.9 %collective-permute-start.7 = (f32[1,3,2,64,128]{4,3,2,1,0:T(8,128)}, f32[1,3,2,64,128]{4,3,2,1,0:T(8,128)}, u32[]{:S(2)}, u32[]{:S(2)}) collective-permute-start(f32[1,3,2,64,128]{4,3,2,1,0:T(8,128)} %get-tuple-element.82), channel_id=1, source_target_pairs={{0,1},{1,2},{2,3},{4,5},{5,6},{6,7},{8,9},{9,10},{10,11},{12,13},{... | collective-permute-start | bytes 589832 | tf_op jit(solution)/shard_map/ppermute | solution.py:27
  54.3 7.2 %copy-start.1 = (f32[1,9,8,64,128]{4,3,2,1,0:T(8,128)S(1)}, f32[1,9,8,64,128]{4,3,2,1,0:T(8,128)}, u32[]{:S(2)}) copy-start(f32[1,9,8,64,128]{4,3,2,1,0:T(8,128)} %param.7) | copy-start | bytes 7077892
  61.5 3.9 %copy-start.7 = (f32[1,3,8,64,128]{4,3,2,1,0:T(8,128)}, f32[1,3,8,64,128]{4,3,2,1,0:T(8,128)S(1)}, u32[]{:S(2)}) copy-start(f32[1,3,8,64,128]{4,3,2,1,0:T(8,128)S(1)} %get-tuple-element.79) | copy-start | bytes 2359300
  61.5 4.8 %copy-start.6 = (f32[1,3,8,64,128]{4,3,2,1,0:T(8,128)}, f32[1,3,8,64,128]{4,3,2,1,0:T(8,128)S(1)}, u32[]{:S(2)}) copy-start(f32[1,3,8,64,128]{4,3,2,1,0:T(8,128)S(1)} %get-tuple-element.78) | copy-start | bytes 2359300
  61.5 4.8 %copy-start.22 = (f32[1,3,8,64,128]{4,3,2,1,0:T(8,128)}, f32[1,3,8,64,128]{4,3,2,1,0:T(8,128)S(1)}, u32[]{:S(2)}) copy-start(f32[1,3,8,64,128]{4,3,2,1,0:T(8,128)S(1)} %get-tuple-element.80) | copy-start | bytes 2359300
  61.5 3.0 copy-start.44
  65.4 15.3 %copy-start.25 = (f32[1,1,8,64,128]{4,3,2,1,0:T(8,128)}, f32[1,1,8,64,128]{4,3,2,1,0:T(8,128)S(1)}, u32[]{:S(2)}) copy-start(f32[1,1,8,64,128]{4,3,2,1,0:T(8,128)S(1)} %get-tuple-element.31) | copy-start | bytes 786436
  66.3 10.0 %copy-start.54 = (s32[4]{0:T(128)S(1)}, s32[4]{0:T(128)}, u32[]{:S(2)}) copy-start(s32[4]{0:T(128)} %param.9) | copy-start | bytes 52
  69.1 12.0 %collective-permute-start.8 = (f32[1,6,2,64,128]{4,3,2,1,0:T(8,128)}, f32[1,6,2,64,128]{4,3,2,1,0:T(8,128)}, u32[]{:S(2)}, u32[]{:S(2)}) collective-permute-start(f32[1,6,2,64,128]{4,3,2,1,0:T(8,128)} %get-tuple-element.60), channel_id=1, source_target_pairs={{0,1},{1,2},{2,3},{4,5},{5,6},{6,7},{8,9},{9,10},{10,11},{12,13},{... | collective-permute-start | bytes 1179656 | tf_op jit(solution)/shard_map/ppermute | solution.py:27
  75.0 6.2 %collective-permute-start.9 = (f32[1,6,2,64,128]{4,3,2,1,0:T(8,128)}, f32[1,6,2,64,128]{4,3,2,1,0:T(8,128)}, u32[]{:S(2)}, u32[]{:S(2)}) collective-permute-start(f32[1,6,2,64,128]{4,3,2,1,0:T(8,128)} %get-tuple-element.61), channel_id=1, source_target_pairs={{1,0},{2,1},{3,2},{5,4},{6,5},{7,6},{9,8},{10,9},{11,10},{13,12},{... | collective-permute-start | bytes 1179656 | tf_op jit(solution)/shard_map/ppermute | solution.py:28
  83.5 10.2 %copy-start.49 = (bf16[1,6,8,64,128]{4,3,2,1,0:T(8,128)(2,1)S(1)}, bf16[1,6,8,64,128]{4,3,2,1,0:T(8,128)(2,1)}, u32[]{:S(2)}) copy-start(bf16[1,6,8,64,128]{4,3,2,1,0:T(8,128)(2,1)} %param.8) | copy-start | bytes 2359300
  84.2 11.2 %copy-start.16 = (f32[1,3,8,64,128]{4,3,2,1,0:T(8,128)}, f32[1,3,8,64,128]{4,3,2,1,0:T(8,128)S(1)}, u32[]{:S(2)}) copy-start(f32[1,3,8,64,128]{4,3,2,1,0:T(8,128)S(1)} %fusion.90) | copy-start | bytes 2359300
  85.0 10.6 %collective-permute-start.10 = (f32[1,3,2,64,128]{4,3,2,1,0:T(8,128)}, f32[1,3,2,64,128]{4,3,2,1,0:T(8,128)}, u32[]{:S(2)}, u32[]{:S(2)}) collective-permute-start(f32[1,3,2,64,128]{4,3,2,1,0:T(8,128)} %get-tuple-element.76), channel_id=1, source_target_pairs={{1,0},{2,1},{3,2},{5,4},{6,5},{7,6},{9,8},{10,9},{11,10},{13,12},{... | collective-permute-start | bytes 589832 | tf_op jit(solution)/shard_map/ppermute | solution.py:28
  86.3 9.4 %collective-permute-start.11 = (f32[1,3,2,64,128]{4,3,2,1,0:T(8,128)}, f32[1,3,2,64,128]{4,3,2,1,0:T(8,128)}, u32[]{:S(2)}, u32[]{:S(2)}) collective-permute-start(f32[1,3,2,64,128]{4,3,2,1,0:T(8,128)} %get-tuple-element.77), channel_id=1, source_target_pairs={{0,1},{1,2},{2,3},{4,5},{5,6},{6,7},{8,9},{9,10},{10,11},{12,13},{... | collective-permute-start | bytes 589832 | tf_op jit(solution)/shard_map/ppermute | solution.py:27
  95.4 6.6 %copy-start.47 = (f32[1,1,8,64,128]{4,3,2,1,0:T(8,128)S(1)}, f32[1,1,8,64,128]{4,3,2,1,0:T(8,128)}, u32[]{:S(2)}) copy-start(f32[1,1,8,64,128]{4,3,2,1,0:T(8,128)} %get-tuple-element.37) | copy-start | bytes 786436
  95.5 200.8 %reduce-scatter.3.cloned.1.call-start = ((), (), s32[]{:S(2)}) async-start(), calls=%async_computation.2 | async-start | bytes 294912 | tf_op jit(solution)/shard_map/reduce_scatter | solution.py:131
  102.1 2.5 copy-start.8
  102.1 27.1 %copy-start.10 = (f32[1,3,8,64,128]{4,3,2,1,0:T(8,128)}, f32[1,3,8,64,128]{4,3,2,1,0:T(8,128)S(1)}, u32[]{:S(2)}) copy-start(f32[1,3,8,64,128]{4,3,2,1,0:T(8,128)S(1)} %get-tuple-element.75) | copy-start | bytes 2359300
  104.6 6.0 %copy-start.29 = (f32[1,1,8,64,128]{4,3,2,1,0:T(8,128)}, f32[1,1,8,64,128]{4,3,2,1,0:T(8,128)S(1)}, u32[]{:S(2)}) copy-start(f32[1,1,8,64,128]{4,3,2,1,0:T(8,128)S(1)} %get-tuple-element.17) | copy-start | bytes 786436
  105.3 5.3 %copy-start.31 = (f32[1,1,8,64,128]{4,3,2,1,0:T(8,128)}, f32[1,1,8,64,128]{4,3,2,1,0:T(8,128)S(1)}, u32[]{:S(2)}) copy-start(f32[1,1,8,64,128]{4,3,2,1,0:T(8,128)S(1)} %get-tuple-element.15) | copy-start | bytes 786436
  105.3 5.8 %collective-permute-start.12 = (f32[1,6,2,64,128]{4,3,2,1,0:T(8,128)S(1)}, f32[1,6,2,64,128]{4,3,2,1,0:T(8,128)S(1)}, u32[]{:S(2)}, u32[]{:S(2)}) collective-permute-start(f32[1,6,2,64,128]{4,3,2,1,0:T(8,128)S(1)} %get-tuple-element.58), channel_id=1, source_target_pairs={{0,1},{1,2},{2,3},{4,5},{5,6},{6,7},{8,9},{9,10},{10,11},{12,13},{... | collective-permute-start | bytes 1179656 | tf_op jit(solution)/shard_map/ppermute | solution.py:27
  109.2 5.6 %collective-permute-start.13 = (f32[1,6,2,64,128]{4,3,2,1,0:T(8,128)S(1)}, f32[1,6,2,64,128]{4,3,2,1,0:T(8,128)S(1)}, u32[]{:S(2)}, u32[]{:S(2)}) collective-permute-start(f32[1,6,2,64,128]{4,3,2,1,0:T(8,128)S(1)} %get-tuple-element.59), channel_id=1, source_target_pairs={{1,0},{2,1},{3,2},{5,4},{6,5},{7,6},{9,8},{10,9},{11,10},{13,12},{... | collective-permute-start | bytes 1179656 | tf_op jit(solution)/shard_map/ppermute | solution.py:28
  111.1 3.8 %copy-start.17 = (f32[1,3,8,64,128]{4,3,2,1,0:T(8,128)S(1)}, f32[1,3,8,64,128]{4,3,2,1,0:T(8,128)}, u32[]{:S(2)}) copy-start(f32[1,3,8,64,128]{4,3,2,1,0:T(8,128)} %copy-done.16) | copy-start | bytes 2359300
  116.5 10.4 %collective-permute-start.14 = (f32[1,3,2,64,128]{4,3,2,1,0:T(8,128)S(1)}, f32[1,3,2,64,128]{4,3,2,1,0:T(8,128)S(1)}, u32[]{:S(2)}, u32[]{:S(2)}) collective-permute-start(f32[1,3,2,64,128]{4,3,2,1,0:T(8,128)S(1)} %get-tuple-element.71), channel_id=1, source_target_pairs={{1,0},{2,1},{3,2},{5,4},{6,5},{7,6},{9,8},{10,9},{11,10},{13,12},{... | collective-permute-start | bytes 589832 | tf_op jit(solution)/shard_map/ppermute | solution.py:28
  117.8 11.4 %copy-start.48 = (f32[1,1,8,64,128]{4,3,2,1,0:T(8,128)S(1)}, f32[1,1,8,64,128]{4,3,2,1,0:T(8,128)}, u32[]{:S(2)}) copy-start(f32[1,1,8,64,128]{4,3,2,1,0:T(8,128)} %get-tuple-element.37) | copy-start | bytes 786436
  117.8 10.1 %collective-permute-start.15 = (f32[1,3,2,64,128]{4,3,2,1,0:T(8,128)S(1)}, f32[1,3,2,64,128]{4,3,2,1,0:T(8,128)S(1)}, u32[]{:S(2)}, u32[]{:S(2)}) collective-permute-start(f32[1,3,2,64,128]{4,3,2,1,0:T(8,128)S(1)} %get-tuple-element.72), channel_id=1, source_target_pairs={{0,1},{1,2},{2,3},{4,5},{5,6},{6,7},{8,9},{9,10},{10,11},{12,13},{... | collective-permute-start | bytes 589832 | tf_op jit(solution)/shard_map/ppermute | solution.py:27
  226.9 2.7 copy-start.12
  227.1 2.5 copy-start.13
  234.6 127.0 %reduce-scatter.5.cloned.1.call-start = ((), (), s32[]{:S(2)}) async-start(), calls=%async_computation.3 | async-start | bytes 294912 | tf_op jit(solution)/shard_map/reduce_scatter | solution.py:132
  242.1 3.6 copy-start.32
  (30 other events, 45.9 us)
Sparse Core Ops, SparseCore 0:
  95.6 129.9 all-reduce.18
  234.8 61.4 reduce-scatter.2
  300.2 61.4 reduce-scatter.4
where the time goes:
time: 369 us; the launch traced here: 368 us
  waiting for transfers between devices  220 us (60%)
  starting transfers between devices  62.2 us (17%)
  other arithmetic  53.6 us (15%)
  between operations  17.3 us (5%)
  local copies, waits for them, and re-layouts  15.3 us (4%)
    psum x1, waiting for transfers between devices, spread(): return lax.psum(block, axis)  93.7 us
    reduce_scatter x1, waiting for transfers between devices, local(): lax.psum_scatter(kernel_mu, 'src', scatter_dimension=1, tiled=True)  65.4 us
    ppermute x8, starting transfers between devices, extended(): before = lax.ppermute(last, axis, up)  51.6 us
    reduce_scatter x1, waiting for transfers between devices, local(): lax.psum_scatter(kernel_lambda, 'src', scatter_dimension=1, tiled=True)  48.8 us
    div x4, other arithmetic, diff_valid(): return (8.0 * near - far) / 12.0  15.3 us
    unnamed x21, other arithmetic  13.4 us
    ppermute x8, starting transfers between devices, extended(): after = lax.ppermute(initial, axis, down)  10.3 us
    unnamed x116, local copies, waits for them, and re-layouts  9.34 us
  transfers between devices with their start and end apart: 19, of which 9 were waited for; matrix products, arithmetic and copies ran while one was open for 9% of the time, Pallas kernels for 0%

commit v1 on v0

v1 whole, which is shorter than its diff:
```python
import functools

import jax
import jax.numpy as jnp
from jax import lax
from jax.experimental import pallas as pl
from jax.experimental.pallas import tpu as pltpu
from jax.sharding import PartitionSpec as P

STEPS = 4
DT = 0.3
NEAR = 8.0 / 12.0
FAR = 1.0 / 12.0
MESH = pl.DeviceIdType.MESH

XX, XZ, XY, YY, ZZ, YZ = range(6)
BANK = (0, 4, 5, 1, 2, 3)
PAD = 8


def kernel(
    n, m, nx, ny, chunk, split,
    owners, t_lam, t_mu, t_buoy, region, wave, bank,
    out_wave, out_lam, out_mu,
    vel, sig, mat, swap, gather, terms, arrived,
    load_sem, store_sem, bank_sem,
    a2a_send, a2a_recv, g_send, g_recv, k_send, k_recv,
    vs_send, vs_recv, ss_send, ss_recv,
):
    me = lax.axis_index("src")
    pos = lax.axis_index("space")
    rows = ny // n
    first, last = pos == 0, pos == m - 1
    lower, upper = lax.rem(pos + m - 1, m), lax.rem(pos + 1, m)

    inside = (slice(2, 2 + nx), slice(PAD, PAD + ny))
    loads = []
    for src, dst in (
        (wave.at[3:4], sig.at[0, XX:XZ, inside[0], inside[1]]),
        (wave.at[7:9], sig.at[0, XZ:YY, inside[0], inside[1]]),
        (wave.at[4:7], sig.at[0, YY:, inside[0], inside[1]]),
        (wave.at[0:3], vel.at[0, :, inside[0], inside[1]]),
    ):
        loads.append(pltpu.make_async_copy(src, dst, load_sem.at[len(loads)]))
        loads[-1].start()
    own = pltpu.make_async_copy(bank.at[:, me], swap.at[me], bank_sem)
    own.start()

    barrier = pltpu.get_barrier_semaphore()
    for d in range(1, n):
        pl.semaphore_signal(barrier, inc=1, device_id={"src": lax.rem(me + d, n)}, device_id_type=MESH)
    for to in (lower, upper):
        pl.semaphore_signal(barrier, inc=1, device_id={"space": to}, device_id_type=MESH)
    pl.semaphore_wait(barrier, n - 1 + 2)

    swaps = []
    for d in range(1, n):
        peer = lax.rem(me + d, n)
        swaps.append(pltpu.make_async_remote_copy(
            src_ref=bank.at[:, peer], dst_ref=swap.at[me],
            send_sem=a2a_send.at[d], recv_sem=a2a_recv.at[d],
            device_id={"src": peer}, device_id_type=MESH))

    def halos(buf, t, send, recv):
        down = pltpu.make_async_remote_copy(
            src_ref=buf.at[t, 0:3, 2:4, inside[1]],
            dst_ref=buf.at[t, 0:3, nx + 2:nx + 4, inside[1]],
            send_sem=send.at[t, 0], recv_sem=recv.at[t, 0],
            device_id={"space": lower}, device_id_type=MESH)
        up = pltpu.make_async_remote_copy(
            src_ref=buf.at[t, 0:3, nx:nx + 2, inside[1]],
            dst_ref=buf.at[t, 0:3, 0:2, inside[1]],
            send_sem=send.at[t, 1], recv_sem=recv.at[t, 1],
            device_id={"space": upper}, device_id_type=MESH)
        return down, up

    def send_halos(pair):
        pl.when(jnp.logical_not(first))(lambda: pair[0].start())
        pl.when(jnp.logical_not(last))(lambda: pair[1].start())

    def take_halos(pair):
        pl.when(jnp.logical_not(last))(lambda: pair[0].wait_recv())
        pl.when(jnp.logical_not(first))(lambda: pair[1].wait_recv())

    def sent_halos(pair):
        pl.when(jnp.logical_not(first))(lambda: pair[0].wait_send())
        pl.when(jnp.logical_not(last))(lambda: pair[1].wait_send())

    s_halos = [halos(sig, t, ss_send, ss_recv) for t in range(STEPS)]
    v_halos = [halos(vel, t, vs_send, vs_recv) for t in range(1, STEPS + 1)]

    for copy in loads[:2]:
        copy.wait()
    send_halos(s_halos[0])
    for copy in swaps:
        copy.start()

    wide = vel.shape[-1]
    for buf, times in ((sig, range(STEPS)), (vel, range(1, STEPS + 1))):
        for t in times:
            count = buf.shape[1]
            edge = jnp.zeros((count, nx, PAD, wide), jnp.float32)
            buf[t, :, 2:nx + 2, 0:PAD, :] = edge
            buf[t, :, 2:nx + 2, PAD + ny:, :] = edge

            @pl.when(first)
            def _():
                buf[t, 0:3, 0:2, PAD:PAD + ny, :] = jnp.zeros((3, 2, ny, wide), jnp.float32)

            @pl.when(last)
            def _():
                buf[t, 0:3, nx + 2:, PAD:PAD + ny, :] = jnp.zeros((3, 2, ny, wide), jnp.float32)

    def materials(i, carry):
        label = region[i]
        found = [jnp.zeros(label.shape, jnp.float32) for _ in range(3)]
        for which in range(t_lam.shape[0]):
            hit = label == which
            found = [jnp.where(hit, table[which], old)
                     for table, old in zip((t_lam, t_mu, t_buoy), found)]
        for which in range(3):
            mat[which, i] = found[which]
        return carry

    lax.fori_loop(0, nx, materials, 0)
    for copy in loads[2:]:
        copy.wait()

    tall = ny // split
    lane = lax.broadcasted_iota(jnp.int32, (tall, wide), 1)

    def deriv_x(buf, t, c, i, y):
        at = lambda k: buf[t, c, i + 2 + k, PAD + y:PAD + y + tall, :]
        return at(1) - at(-1), at(2) - at(-2)

    def deriv_y(buf, t, c, i, y):
        at = lambda k: buf[t, c, i + 2, PAD + y + k:PAD + y + k + tall, :]
        return at(1) - at(-1), at(2) - at(-2)

    def deriv_z(buf, t, c, i, y):
        f = buf[t, c, i + 2, PAD + y:PAD + y + tall, :]

        def at(k):
            moved = pltpu.roll(f, (-k) % wide, 1)
            keep = lane < wide - k if k > 0 else lane >= -k
            return jnp.where(keep, moved, 0.0)

        return at(1) - at(-1), at(2) - at(-2)

    def total(*pairs):
        near, far = pairs[0]
        for a, b in pairs[1:]:
            near, far = near + a, far + b
        return NEAR * near - FAR * far

    def velocity_row(t, i):
        for y in range(0, ny, tall):
            here = slice(PAD + y, PAD + y + tall)
            gain = DT * mat[2, i, y:y + tall, :]
            for c, (a, b, d) in enumerate(((XX, XY, XZ), (XY, YY, YZ), (XZ, YZ, ZZ))):
                force = total(deriv_x(sig, t, a, i, y), deriv_y(sig, t, b, i, y), deriv_z(sig, t, d, i, y))
                vel[t + 1, c, i + 2, here, :] = vel[t, c, i + 2, here, :] + gain * force

    def stress_row(t, i):
        s = t + 1
        for y in range(0, ny, tall):
            here = slice(PAD + y, PAD + y + tall)
            lam = DT * mat[0, i, y:y + tall, :]
            mu = DT * mat[1, i, y:y + tall, :]

            def put(c, change):
                sig[s, c, i + 2, here, :] = sig[t, c, i + 2, here, :] + change

            gx = total(deriv_x(vel, s, 0, i, y))
            gy = total(deriv_y(vel, s, 1, i, y))
            gz = total(deriv_z(vel, s, 2, i, y))
            div = lam * (gx + gy + gz)
            put(XX, div + 2.0 * mu * gx)
            put(YY, div + 2.0 * mu * gy)
            put(ZZ, div + 2.0 * mu * gz)
            put(YZ, mu * total(deriv_z(vel, s, 1, i, y), deriv_y(vel, s, 2, i, y)))
            put(XZ, mu * total(deriv_z(vel, s, 0, i, y), deriv_x(vel, s, 2, i, y)))
            put(XY, mu * total(deriv_y(vel, s, 0, i, y), deriv_x(vel, s, 1, i, y)))

    def over(row, t, start, stop):
        def body(i, carry):
            row(t, i)
            return carry
        lax.fori_loop(start, stop, body, 0)

    spreads = []
    for d in range(1, n):
        peer = lax.rem(me + d, n)
        spreads.append(pltpu.make_async_remote_copy(
            src_ref=gather.at[me], dst_ref=gather.at[me],
            send_sem=g_send.at[d], recv_sem=g_recv.at[d],
            device_id={"src": peer}, device_id_type=MESH))

    for t in range(STEPS):
        over(velocity_row, t, 2, nx - 2)
        take_halos(s_halos[t])
        over(velocity_row, t, 0, 2)
        over(velocity_row, t, nx - 2, nx)
        send_halos(v_halos[t])
        over(stress_row, t, 2, nx - 2)
        if t == 0:
            own.wait()
            for copy in swaps:
                copy.wait()
            for s in range(STEPS):
                gather[me, s] = swap[owners[s]]
            for copy in spreads:
                copy.start()
        take_halos(v_halos[t])
        over(stress_row, t, 0, 2)
        over(stress_row, t, nx - 2, nx)
        if t + 1 < STEPS:
            send_halos(s_halos[t + 1])

    stores = []
    for src, dst in (
        (sig.at[STEPS, XX:XZ, inside[0], inside[1]], out_wave.at[3:4]),
        (sig.at[STEPS, XZ:YY, inside[0], inside[1]], out_wave.at[7:9]),
        (sig.at[STEPS, YY:, inside[0], inside[1]], out_wave.at[4:7]),
        (vel.at[STEPS, :, inside[0], inside[1]], out_wave.at[0:3]),
    ):
        stores.append(pltpu.make_async_copy(src, dst, store_sem.at[len(stores)]))
        stores[-1].start()

    for copy in spreads:
        copy.wait()

    per_row = ny // chunk

    def correlate(i, carry):
        for part in range(per_row):
            y = part * chunk
            j = i * per_row + part
            lam = mat[0, i, y:y + chunk, :]
            mu = mat[1, i, y:y + chunk, :]
            stiff = 1.0 / (3.0 * lam + 2.0 * mu)
            soft = DT / mu
            k_lam = jnp.zeros(lam.shape, jnp.float32)
            k_mu = jnp.zeros(lam.shape, jnp.float32)
            for t in range(STEPS):
                s = [sig[t + 1, c, i + 2, PAD + y:PAD + y + chunk, :] for c in range(6)]
                r = [gather[j, t, BANK[c]].astype(jnp.float32) for c in range(6)]
                theta = (s[XX] + s[YY] + s[ZZ]) * stiff
                trace = theta * (r[XX] + r[YY] + r[ZZ])
                k_lam = k_lam + trace
                k_mu = (k_mu + s[XX] * r[XX] + s[YY] * r[YY] + s[ZZ] * r[ZZ] - lam * trace
                        + 2.0 * (s[YZ] * r[YZ] + s[XZ] * r[XZ] + s[XY] * r[XY]))
            k_lam = DT * k_lam
            k_mu = soft * k_mu
            for z in range(chunk // rows):
                terms[y // rows + z, 0, i] = k_lam[z * rows:(z + 1) * rows]
                terms[y // rows + z, 1, i] = k_mu[z * rows:(z + 1) * rows]
        return carry

    lax.fori_loop(0, nx, correlate, 0)

    sums = []
    for d in range(1, n):
        peer = lax.rem(me + d, n)
        sums.append(pltpu.make_async_remote_copy(
            src_ref=terms.at[peer], dst_ref=arrived.at[me],
            send_sem=k_send.at[d], recv_sem=k_recv.at[d],
            device_id={"src": peer}, device_id_type=MESH))
        sums[-1].start()
    for pair in s_halos + v_halos:
        sent_halos(pair)
    arrived[me] = terms[me]
    for copy in sums:
        copy.wait()
    for which, out in ((0, out_lam), (1, out_mu)):
        acc = arrived[0, which]
        for d in range(1, n):
            acc = acc + arrived[d, which]
        out[...] = acc
    for copy in stores:
        copy.wait()


def solution(mesh):
    n, m = mesh.shape["src"], mesh.shape["space"]

    def local(wavefield, strain_bank, owners, region, region_lambda, region_mu, region_buoyancy):
        nx, ny, nz = region.shape
        chunk = nx * ny // n
        rows = ny // n
        bank = strain_bank[0].reshape(6, n, chunk, nz)
        hbm = pl.BlockSpec(memory_space=pl.ANY)
        vmem = pl.BlockSpec(memory_space=pltpu.VMEM)
        smem = pl.BlockSpec(memory_space=pltpu.SMEM)
        dma = pltpu.SemaphoreType.DMA
        new, k_lam, k_mu = pl.pallas_call(
            functools.partial(kernel, n, m, nx, ny, chunk, 2),
            out_shape=(
                jax.ShapeDtypeStruct((9, nx, ny, nz), jnp.float32),
                jax.ShapeDtypeStruct((nx, rows, nz), jnp.float32),
                jax.ShapeDtypeStruct((nx, rows, nz), jnp.float32),
            ),
            in_specs=[smem, smem, smem, smem, vmem, hbm, hbm],
            out_specs=(hbm, vmem, vmem),
            scratch_shapes=[
                pltpu.VMEM((STEPS + 1, 3, nx + 4, ny + 2 * PAD, nz), jnp.float32),
                pltpu.VMEM((STEPS + 1, 6, nx + 4, ny + 2 * PAD, nz), jnp.float32),
                pltpu.VMEM((3, nx, ny, nz), jnp.float32),
                pltpu.VMEM((n, 6, chunk, nz), jnp.bfloat16),
                pltpu.VMEM((n, STEPS, 6, chunk, nz), jnp.bfloat16),
                pltpu.VMEM((n, 2, nx, rows, nz), jnp.float32),
                pltpu.VMEM((n, 2, nx, rows, nz), jnp.float32),
                dma((4,)), dma((4,)), dma,
                dma((n,)), dma((n,)), dma((n,)), dma((n,)), dma((n,)), dma((n,)),
                dma((STEPS + 1, 2)), dma((STEPS + 1, 2)), dma((STEPS + 1, 2)), dma((STEPS + 1, 2)),
            ],
            compiler_params=pltpu.CompilerParams(
                collective_id=0, has_side_effects=True, vmem_limit_bytes=56 * 1024 * 1024
            ),
        )(owners, region_lambda, region_mu, region_buoyancy, region, wavefield[0], bank)
        return new[None], k_lam, k_mu

    in_specs = (
        P("src", None, "space", None, None),
        P("src", None, "space", None, None),
        P(),
        P("space", None, None),
        P(),
        P(),
        P(),
    )
    out_specs = (
        P("src", None, "space", None, None),
        P("space", "src", None),
        P("space", "src", None),
    )
    return jax.shard_map(local, mesh=mesh, in_specs=in_specs, out_specs=out_specs, check_vma=False)
```

time: 369 us -> 116 us (0.31)
  waiting for transfers between devices: 220 us -> 0 us
  Pallas kernels: 0 us -> 108 us
  starting transfers between devices: 62.2 us -> 0 us
  other arithmetic: 53.6 us -> 0 us
  between operations: 17.3 us -> 0.66 us
  local copies, waits for them, and re-layouts: 15.3 us -> 4.61 us
    reduce_scatter x2 -> x0, waiting for transfers between devices: 114 us -> none  [the longest x1 65.4 us: local(): lax.psum_scatter(kernel_mu, 'src', scatter_dimension=1, tiled=True)]
    pallas_call x0 -> x1, Pallas kernels: none -> 108 us  [local(): pl.pallas_call(functools.partial(kernel, n, m, nx, ny, chunk, 2), out_sha...]
    psum x1 -> x0, waiting for transfers between devices: 93.7 us -> none  [spread(): return lax.psum(block, axis)]
    ppermute x16 -> x0, starting transfers between devices: 61.9 us -> none  [the longest x8 51.6 us: extended(): before = lax.ppermute(last, axis, up)]
    div x4 -> x0, other arithmetic: 15.3 us -> none  [diff_valid(): return (8.0 * near - far) / 12.0]
    unnamed x21 -> x0, other arithmetic: 13.4 us -> none
    add x5 -> x0, other arithmetic: 13.1 us -> none  [the longest x1 7.43 us: local(): kernel_mu = kernel_mu + jnp.sum(term_mu, 0)]
    ppermute x16 -> x0, waiting for transfers between devices: 11.9 us -> none  [the longest x8 9.13 us: extended(): after = lax.ppermute(initial, axis, down)]
  transfers between devices with their start and end apart: 19 -> 0, of which waited for: 9 -> 0; matrix products, arithmetic and copies ran while one was open for 9% -> 0% of each run, Pallas kernels for 0% -> 0%
where the time goes in v1:
time: 116 us; the launch traced here: 113 us
  Pallas kernels  108 us (93%)
  local copies, waits for them, and re-layouts  4.61 us (4%)
    pallas_call x1, Pallas kernels, local(): pl.pallas_call(functools.partial(kernel, n, m, nx, ny, chunk, 2), out_sha...  108 us
    unnamed x7, local copies, waits for them, and re-layouts  4.61 us

profile of v1, /device:TPU:0, one launch (start us, length us, event | category | flops | bytes accessed | tf_op | source)
XLA Modules:
  0.0 113.5 jit_solution(10451875129446871529)
XLA Ops:
  0.6 108.2 %shard_map.94 = (f32[9,8,64,128]{3,2,1,0:T(8,128)}, f32[8,8,128]{2,1,0:T(8,128)}, f32[8,8,128]{2,1,0:T(8,128)}) custom-call(s32[4]{0:T(128)} %owners.1, f32[8]{0:T(128)} %t_lam.1, f32[8]{0:T(128)} %t_mu.1, f32[8]{0:T(128)} %t_buoy.1, s32[8,64,128]{2,1,0:T(8,128)} %region.1, f32[9,8,64,128]{3,2,1,0:T(8,128)} %bitcast.3, bf16[6,8,64,128]{3,2,1,0:T(8,128)(2,1)} %bitcast.5), custom_call_target="tpu_custom_call" | custom-call | tf_op jit(solution)/shard_map/pallas_call | solution.py:296
  108.9 0.0 copy-start.1
  108.9 0.0 copy-start
  108.9 3.4 %copy.13 = f32[1,9,8,64,128]{4,3,2,1,0:T(8,128)} copy(f32[1,9,8,64,128]{4,3,2,1,0:T(8,128)} %bitcast.4) | data formatting | bytes 4718592
  112.3 0.0 copy-done.1
  112.3 0.6 copy.14
  112.9 0.0 copy-done
  112.9 0.6 copy.15
Async XLA Ops:
  108.9 3.4 %copy-start.1 = (f32[8,8,128]{2,1,0:T(8,128)S(1)}, f32[8,8,128]{2,1,0:T(8,128)}, u32[]{:S(2)}) copy-start(f32[8,8,128]{2,1,0:T(8,128)} %get-tuple-element.13) | copy-start | bytes 98308
  108.9 4.0 %copy-start = (f32[8,8,128]{2,1,0:T(8,128)S(1)}, f32[8,8,128]{2,1,0:T(8,128)}, u32[]{:S(2)}) copy-start(f32[8,8,128]{2,1,0:T(8,128)} %get-tuple-element.14) | copy-start | bytes 98308

commit v2 on v1

--- a/solution.py
+++ b/solution.py
@@ -24,7 +24,7 @@
     out_wave, out_lam, out_mu,
     vel, sig, mat, swap, gather, terms, arrived,
     load_sem, store_sem, bank_sem,
-    a2a_send, a2a_recv, g_send, g_recv, k_send, k_recv,
+    a2a_send, a2a_recv, c_send, c_recv, p_send, p_recv, b_send, b_recv, k_send, k_recv,
     vs_send, vs_recv, ss_send, ss_recv,
 ):
     me = lax.axis_index("src")
@@ -188,13 +188,106 @@
             return carry
         lax.fori_loop(start, stop, body, 0)
 
-    spreads = []
-    for d in range(1, n):
-        peer = lax.rem(me + d, n)
-        spreads.append(pltpu.make_async_remote_copy(
-            src_ref=gather.at[me], dst_ref=gather.at[me],
-            send_sem=g_send.at[d], recv_sem=g_recv.at[d],
-            device_id={"src": peer}, device_id_type=MESH))
+    line, side = me // 2, lax.rem(me, 2)
+    lines = n // 2
+    partner = me + 1 - 2 * side
+    ways = (1, -1)
+    most, rest = pl.ds(0, STEPS - 1), pl.ds(STEPS - 1, 1)
+    items = ((most, False), (rest, False), (rest, True))
+
+    def place(origin, swapped):
+        return origin * 2 + (1 - side if swapped else side)
+
+    def link(k, w, hop, origin):
+        slots, swapped = items[k]
+        part = gather.at[place(origin, swapped), slots]
+        return pltpu.make_async_remote_copy(
+            src_ref=part, dst_ref=part,
+            send_sem=c_send.at[k, w, hop], recv_sem=c_recv.at[k, w, hop],
+            device_id={"src": me + 2 * ways[w]}, device_id_type=MESH)
+
+    def across(w, hop, origin):
+        part = gather.at[place(origin, False), most]
+        other = gather.at[place(origin, True), most]
+        send = pltpu.make_async_remote_copy(
+            src_ref=part, dst_ref=part, send_sem=p_send.at[w, hop], recv_sem=p_recv.at[w, hop],
+            device_id={"src": partner}, device_id_type=MESH)
+        take = pltpu.make_async_remote_copy(
+            src_ref=other, dst_ref=other, send_sem=p_send.at[w, hop], recv_sem=p_recv.at[w, hop],
+            device_id={"src": partner}, device_id_type=MESH)
+        return send, take
+
+    def across_rest(whose):
+        part = gather.at[whose, rest]
+        return pltpu.make_async_remote_copy(
+            src_ref=part, dst_ref=part, send_sem=b_send, recv_sem=b_recv,
+            device_id={"src": partner}, device_id_type=MESH)
+
+    def exists(at):
+        return jnp.logical_and(at >= 0, at < lines)
+
+    def each_link(k, hop, act):
+        for w, way in enumerate(ways):
+            origin = line - way * hop
+            pl.when(jnp.logical_and(exists(origin), exists(line + way)))(
+                lambda w=w, origin=origin: act(link(k, w, hop, origin)))
+
+    def take_link(k, hop):
+        for w, way in enumerate(ways):
+            origin = line - way * (hop + 1)
+            pl.when(exists(origin))(lambda w=w, origin=origin: link(k, w, hop, origin).wait_recv())
+
+    def each_across(hop, act):
+        for w, way in enumerate(ways):
+            origin = line - way * (hop + 1)
+            pl.when(exists(origin))(lambda w=w, origin=origin: act(*across(w, hop + 1, origin)))
+
+    start = lambda copy: copy.start()
+
+    def begin():
+        own.wait()
+        for copy in swaps:
+            copy.wait()
+        for s in range(STEPS):
+            gather[me, s] = swap[owners[s]]
+        across_rest(me).start()
+        each_link(0, 0, start)
+        across(0, 0, line)[0].start()
+        each_link(1, 0, start)
+
+    def along_most(hop):
+        if hop == 0:
+            across_rest(partner).wait_recv()
+            each_link(2, 0, start)
+        take_link(0, hop)
+        if hop + 1 < lines - 1:
+            each_link(0, hop + 1, start)
+        each_across(hop, lambda send, take: send.start())
+
+    def along_rest(hop):
+        for k in (1, 2):
+            take_link(k, hop)
+            if hop + 1 < lines - 1:
+                each_link(k, hop + 1, start)
+
+    def settle(send, take):
+        send.wait_send()
+        take.wait_recv()
+
+    def finish():
+        across_rest(me).wait_send()
+        send, take = across(0, 0, line)
+        send.wait_send()
+        take.wait_recv()
+        for hop in range(lines - 1):
+            for k in range(3):
+                each_link(k, hop, lambda copy: copy.wait_send())
+            each_across(hop, settle)
+
+    pumps = [begin]
+    for hop in range(lines - 1):
+        pumps.append(functools.partial(along_most, hop))
+        pumps.append(functools.partial(along_rest, hop))
 
     for t in range(STEPS):
         over(velocity_row, t, 2, nx - 2)
@@ -202,20 +295,15 @@
         over(velocity_row, t, 0, 2)
         over(velocity_row, t, nx - 2, nx)
         send_halos(v_halos[t])
+        if t > 0:
+            pumps.pop(0)()
         over(stress_row, t, 2, nx - 2)
-        if t == 0:
-            own.wait()
-            for copy in swaps:
-                copy.wait()
-            for s in range(STEPS):
-                gather[me, s] = swap[owners[s]]
-            for copy in spreads:
-                copy.start()
         take_halos(v_halos[t])
         over(stress_row, t, 0, 2)
         over(stress_row, t, nx - 2, nx)
         if t + 1 < STEPS:
             send_halos(s_halos[t + 1])
+            pumps.pop(0)()
 
     stores = []
     for src, dst in (
@@ -227,8 +315,9 @@
         stores.append(pltpu.make_async_copy(src, dst, store_sem.at[len(stores)]))
         stores[-1].start()
 
-    for copy in spreads:
-        copy.wait()
+    for pump in pumps:
+        pump()
+    finish()
 
     per_row = ny // chunk
 
@@ -311,7 +400,8 @@
                 pltpu.VMEM((n, 2, nx, rows, nz), jnp.float32),
                 pltpu.VMEM((n, 2, nx, rows, nz), jnp.float32),
                 dma((4,)), dma((4,)), dma,
-                dma((n,)), dma((n,)), dma((n,)), dma((n,)), dma((n,)), dma((n,)),
+                dma((n,)), dma((n,)), dma((3, 2, n // 2)), dma((3, 2, n // 2)),
+                dma((2, n // 2)), dma((2, n // 2)), dma, dma, dma((n,)), dma((n,)),
                 dma((STEPS + 1, 2)), dma((STEPS + 1, 2)), dma((STEPS + 1, 2)), dma((STEPS + 1, 2)),
             ],
             compiler_params=pltpu.CompilerParams(

time: 116 us -> 79.3 us (0.68); the launches traced: 113 us -> 78.9 us
  Pallas kernels: 108 us -> 73.6 us
    pallas_call x1, Pallas kernels: 108 us -> 73.6 us  [local(): pl.pallas_call(functools.partial(kernel, n, m, nx, ny, chunk, 2), out_sha...]
where the time goes in v2:
time: 79.3 us; the launch traced here: 78.9 us
  Pallas kernels  73.6 us (93%)
  local copies, waits for them, and re-layouts  4.61 us (6%)
    pallas_call x1, Pallas kernels, local(): pl.pallas_call(functools.partial(kernel, n, m, nx, ny, chunk, 2), out_sha...  73.6 us
    unnamed x7, local copies, waits for them, and re-layouts  4.61 us

profile of v2, /device:TPU:0, one launch (start us, length us, event | category | flops | bytes accessed | tf_op | source)
XLA Modules:
  0.0 78.9 jit_solution(9029417211407042579)
XLA Ops:
  0.6 73.6 %shard_map.94 = (f32[9,8,64,128]{3,2,1,0:T(8,128)}, f32[8,8,128]{2,1,0:T(8,128)}, f32[8,8,128]{2,1,0:T(8,128)}) custom-call(s32[4]{0:T(128)} %owners.1, f32[8]{0:T(128)} %t_lam.1, f32[8]{0:T(128)} %t_mu.1, f32[8]{0:T(128)} %t_buoy.1, s32[8,64,128]{2,1,0:T(8,128)} %region.1, f32[9,8,64,128]{3,2,1,0:T(8,128)} %bitcast.3, bf16[6,8,64,128]{3,2,1,0:T(8,128)(2,1)} %bitcast.5), custom_call_target="tpu_custom_call" | custom-call | tf_op jit(solution)/shard_map/pallas_call | solution.py:385
  74.2 0.0 copy-start.1
  74.2 0.0 copy-start
  74.3 3.4 %copy.13 = f32[1,9,8,64,128]{4,3,2,1,0:T(8,128)} copy(f32[1,9,8,64,128]{4,3,2,1,0:T(8,128)} %bitcast.4) | data formatting | bytes 4718592
  77.6 0.0 copy-done.1
  77.6 0.6 copy.14
  78.2 0.0 copy-done
  78.3 0.6 copy.15
Async XLA Ops:
  74.2 3.4 %copy-start.1 = (f32[8,8,128]{2,1,0:T(8,128)S(1)}, f32[8,8,128]{2,1,0:T(8,128)}, u32[]{:S(2)}) copy-start(f32[8,8,128]{2,1,0:T(8,128)} %get-tuple-element.13) | copy-start | bytes 98308
  74.2 4.0 %copy-start = (f32[8,8,128]{2,1,0:T(8,128)S(1)}, f32[8,8,128]{2,1,0:T(8,128)}, u32[]{:S(2)}) copy-start(f32[8,8,128]{2,1,0:T(8,128)} %get-tuple-element.14) | copy-start | bytes 98308

commit v3 on v2

--- a/solution.py
+++ b/solution.py
@@ -61,37 +61,34 @@
             send_sem=a2a_send.at[d], recv_sem=a2a_recv.at[d],
             device_id={"src": peer}, device_id_type=MESH))
 
+    odd = lax.rem(pos, 2)
+    has_far = jnp.where(odd == 1, pos, m - 1 - pos) < m - 1
+    near_rows, far_rows = (1 - odd) * (nx - 2), odd * (nx - 2)
+
     def halos(buf, t, send, recv):
-        down = pltpu.make_async_remote_copy(
-            src_ref=buf.at[t, 0:3, 2:4, inside[1]],
-            dst_ref=buf.at[t, 0:3, nx + 2:nx + 4, inside[1]],
+        near = pltpu.make_async_remote_copy(
+            src_ref=buf.at[t, 0:3, pl.ds(near_rows + 2, 2), inside[1]],
+            dst_ref=buf.at[t, 0:3, pl.ds(odd * (nx + 2), 2), inside[1]],
             send_sem=send.at[t, 0], recv_sem=recv.at[t, 0],
-            device_id={"space": lower}, device_id_type=MESH)
-        up = pltpu.make_async_remote_copy(
-            src_ref=buf.at[t, 0:3, nx:nx + 2, inside[1]],
-            dst_ref=buf.at[t, 0:3, 0:2, inside[1]],
+            device_id={"space": pos + 1 - 2 * odd}, device_id_type=MESH)
+        far = pltpu.make_async_remote_copy(
+            src_ref=buf.at[t, 0:3, pl.ds(far_rows + 2, 2), inside[1]],
+            dst_ref=buf.at[t, 0:3, pl.ds((1 - odd) * (nx + 2), 2), inside[1]],
             send_sem=send.at[t, 1], recv_sem=recv.at[t, 1],
-            device_id={"space": upper}, device_id_type=MESH)
-        return down, up
-
-    def send_halos(pair):
-        pl.when(jnp.logical_not(first))(lambda: pair[0].start())
-        pl.when(jnp.logical_not(last))(lambda: pair[1].start())
-
-    def take_halos(pair):
-        pl.when(jnp.logical_not(last))(lambda: pair[0].wait_recv())
-        pl.when(jnp.logical_not(first))(lambda: pair[1].wait_recv())
+            device_id={"space": lax.rem(pos + m - 1 + 2 * odd, m)}, device_id_type=MESH)
+        return near, far
 
     def sent_halos(pair):
-        pl.when(jnp.logical_not(first))(lambda: pair[0].wait_send())
-        pl.when(jnp.logical_not(last))(lambda: pair[1].wait_send())
+        pair[0].wait_send()
+        pl.when(has_far)(lambda: pair[1].wait_send())
 
     s_halos = [halos(sig, t, ss_send, ss_recv) for t in range(STEPS)]
     v_halos = [halos(vel, t, vs_send, vs_recv) for t in range(1, STEPS + 1)]
 
     for copy in loads[:2]:
         copy.wait()
-    send_halos(s_halos[0])
+    s_halos[0][0].start()
+    pl.when(has_far)(lambda: s_halos[0][1].start())
     for copy in swaps:
         copy.start()
 
@@ -184,9 +181,9 @@
 
     def over(row, t, start, stop):
         def body(i, carry):
-            row(t, i)
+            row(t, start + i)
             return carry
-        lax.fori_loop(start, stop, body, 0)
+        lax.fori_loop(0, nx - 4 if isinstance(start, int) else 2, body, 0)
 
     line, side = me // 2, lax.rem(me, 2)
     lines = n // 2
@@ -270,40 +267,39 @@
             if hop + 1 < lines - 1:
                 each_link(k, hop + 1, start)
 
-    def settle(send, take):
-        send.wait_send()
-        take.wait_recv()
-
     def finish():
         across_rest(me).wait_send()
-        send, take = across(0, 0, line)
-        send.wait_send()
-        take.wait_recv()
+        across(0, 0, line)[0].wait_send()
         for hop in range(lines - 1):
             for k in range(3):
                 each_link(k, hop, lambda copy: copy.wait_send())
-            each_across(hop, settle)
+            each_across(hop, lambda send, take: send.wait_send())
 
     pumps = [begin]
     for hop in range(lines - 1):
         pumps.append(functools.partial(along_most, hop))
         pumps.append(functools.partial(along_rest, hop))
 
+    def phase(row, t, takes, gives):
+        over(row, t, 2, nx - 2)
+        takes[0].wait_recv()
+        over(row, t, near_rows, near_rows + 2)
+        if gives:
+            gives[0].start()
+        pl.when(has_far)(lambda: takes[1].wait_recv())
+        over(row, t, far_rows, far_rows + 2)
+        if gives:
+            pl.when(has_far)(lambda: gives[1].start())
+
     for t in range(STEPS):
-        over(velocity_row, t, 2, nx - 2)
-        take_halos(s_halos[t])
-        over(velocity_row, t, 0, 2)
-        over(velocity_row, t, nx - 2, nx)
-        send_halos(v_halos[t])
-        if t > 0:
+        phase(velocity_row, t, s_halos[t], v_halos[t])
+        if 0 < t < STEPS - 1:
             pumps.pop(0)()
-        over(stress_row, t, 2, nx - 2)
-        take_halos(v_halos[t])
-        over(stress_row, t, 0, 2)
-        over(stress_row, t, nx - 2, nx)
         if t + 1 < STEPS:
-            send_halos(s_halos[t + 1])
+            phase(stress_row, t, v_halos[t], s_halos[t + 1])
             pumps.pop(0)()
+        else:
+            phase(stress_row, t, v_halos[t], None)
 
     stores = []
     for src, dst in (
@@ -315,9 +311,6 @@
         stores.append(pltpu.make_async_copy(src, dst, store_sem.at[len(stores)]))
         stores[-1].start()
 
-    for pump in pumps:
-        pump()
-    finish()
 
     per_row = ny // chunk
 
@@ -346,21 +339,42 @@
                 terms[y // rows + z, 1, i] = k_mu[z * rows:(z + 1) * rows]
         return carry
 
-    lax.fori_loop(0, nx, correlate, 0)
-
-    sums = []
-    for d in range(1, n):
+    group = nx // lines
+
+    def sum_copy(d, g):
         peer = lax.rem(me + d, n)
-        sums.append(pltpu.make_async_remote_copy(
-            src_ref=terms.at[peer], dst_ref=arrived.at[me],
-            send_sem=k_send.at[d], recv_sem=k_recv.at[d],
-            device_id={"src": peer}, device_id_type=MESH))
-        sums[-1].start()
+        part = pl.ds(g * group, group)
+        return pltpu.make_async_remote_copy(
+            src_ref=terms.at[peer, :, part], dst_ref=arrived.at[me, :, part],
+            send_sem=k_send.at[d, g], recv_sem=k_recv.at[d, g],
+            device_id={"src": peer}, device_id_type=MESH)
+
+    def add_group(g):
+        lax.fori_loop(0, group, lambda i, carry: correlate(g * group + i, carry), 0)
+        for d in range(1, n):
+            sum_copy(d, g).start()
+
+    across(0, 0, line)[1].wait_recv()
+    add_group(line)
+    for hop in range(lines - 1):
+        while len(pumps) > 2 * (lines - 2 - hop):
+            pumps.pop(0)()
+        for w, way in enumerate(ways):
+            origin = line - way * (hop + 1)
+
+            def one(w=w, origin=origin):
+                across(w, hop + 1, origin)[1].wait_recv()
+                add_group(origin)
+
+            pl.when(exists(origin))(one)
+    finish()
+
     for pair in s_halos + v_halos:
         sent_halos(pair)
     arrived[me] = terms[me]
-    for copy in sums:
-        copy.wait()
+    for d in range(1, n):
+        for g in range(lines):
+            sum_copy(d, g).wait()
     for which, out in ((0, out_lam), (1, out_mu)):
         acc = arrived[0, which]
         for d in range(1, n):
@@ -401,7 +415,7 @@
                 pltpu.VMEM((n, 2, nx, rows, nz), jnp.float32),
                 dma((4,)), dma((4,)), dma,
                 dma((n,)), dma((n,)), dma((3, 2, n // 2)), dma((3, 2, n // 2)),
-                dma((2, n // 2)), dma((2, n // 2)), dma, dma, dma((n,)), dma((n,)),
+                dma((2, n // 2)), dma((2, n // 2)), dma, dma, dma((n, n // 2)), dma((n, n // 2)),
                 dma((STEPS + 1, 2)), dma((STEPS + 1, 2)), dma((STEPS + 1, 2)), dma((STEPS + 1, 2)),
             ],
             compiler_params=pltpu.CompilerParams(

time: 79.3 us -> 78.9 us (level)
  no operation moved by 1% of the time
where the time goes in v3:
time: 78.9 us; the launch traced here: 78.7 us
  Pallas kernels  73.4 us (93%)
  local copies, waits for them, and re-layouts  4.61 us (6%)
    pallas_call x1, Pallas kernels, local(): pl.pallas_call(functools.partial(kernel, n, m, nx, ny, chunk, 2), out_sha...  73.4 us
    unnamed x7, local copies, waits for them, and re-layouts  4.61 us

profile of v3, /device:TPU:0, one launch (start us, length us, event | category | flops | bytes accessed | tf_op | source)
XLA Modules:
  0.0 78.7 jit_solution(1515297134775110243)
XLA Ops:
  0.6 73.4 %shard_map.94 = (f32[9,8,64,128]{3,2,1,0:T(8,128)}, f32[8,8,128]{2,1,0:T(8,128)}, f32[8,8,128]{2,1,0:T(8,128)}) custom-call(s32[4]{0:T(128)} %owners.1, f32[8]{0:T(128)} %t_lam.1, f32[8]{0:T(128)} %t_mu.1, f32[8]{0:T(128)} %t_buoy.1, s32[8,64,128]{2,1,0:T(8,128)} %region.1, f32[9,8,64,128]{3,2,1,0:T(8,128)} %bitcast.3, bf16[6,8,64,128]{3,2,1,0:T(8,128)(2,1)} %bitcast.5), custom_call_target="tpu_custom_call" | custom-call | tf_op jit(solution)/shard_map/pallas_call | solution.py:399
  74.1 0.0 copy-start.1
  74.1 0.0 copy-start
  74.1 3.4 %copy.13 = f32[1,9,8,64,128]{4,3,2,1,0:T(8,128)} copy(f32[1,9,8,64,128]{4,3,2,1,0:T(8,128)} %bitcast.4) | data formatting | bytes 4718592
  77.5 0.0 copy-done.1
  77.5 0.6 copy.14
  78.1 0.0 copy-done
  78.1 0.6 copy.15
Async XLA Ops:
  74.1 3.4 %copy-start.1 = (f32[8,8,128]{2,1,0:T(8,128)S(1)}, f32[8,8,128]{2,1,0:T(8,128)}, u32[]{:S(2)}) copy-start(f32[8,8,128]{2,1,0:T(8,128)} %get-tuple-element.13) | copy-start | bytes 98308
  74.1 4.0 %copy-start = (f32[8,8,128]{2,1,0:T(8,128)S(1)}, f32[8,8,128]{2,1,0:T(8,128)}, u32[]{:S(2)}) copy-start(f32[8,8,128]{2,1,0:T(8,128)} %get-tuple-element.14) | copy-start | bytes 98308

commit v4 on v3

--- a/solution.py
+++ b/solution.py
@@ -293,7 +293,7 @@
 
     for t in range(STEPS):
         phase(velocity_row, t, s_halos[t], v_halos[t])
-        if 0 < t < STEPS - 1:
+        if t < STEPS - 1:
             pumps.pop(0)()
         if t + 1 < STEPS:
             phase(stress_row, t, v_halos[t], s_halos[t + 1])

time: 78.9 us -> 77.3 us (0.980)
  the two profiles are of different devices: /device:TPU:0 before, /device:TPU:1 now
where the time goes in v4:
time: 77.3 us; the launch traced here: 77.1 us
  Pallas kernels  71.8 us (93%)
  local copies, waits for them, and re-layouts  4.61 us (6%)
    pallas_call x1, Pallas kernels, local(): pl.pallas_call(functools.partial(kernel, n, m, nx, ny, chunk, 2), out_sha...  71.8 us
    unnamed x7, local copies, waits for them, and re-layouts  4.61 us

profile of v4, /device:TPU:1, one launch (start us, length us, event | category | flops | bytes accessed | tf_op | source)
XLA Modules:
  0.0 77.1 jit_solution(12533172443485588807)
XLA Ops:
  0.6 71.8 %shard_map.94 = (f32[9,8,64,128]{3,2,1,0:T(8,128)}, f32[8,8,128]{2,1,0:T(8,128)}, f32[8,8,128]{2,1,0:T(8,128)}) custom-call(s32[4]{0:T(128)} %owners.1, f32[8]{0:T(128)} %t_lam.1, f32[8]{0:T(128)} %t_mu.1, f32[8]{0:T(128)} %t_buoy.1, s32[8,64,128]{2,1,0:T(8,128)} %region.1, f32[9,8,64,128]{3,2,1,0:T(8,128)} %bitcast.3, bf16[6,8,64,128]{3,2,1,0:T(8,128)(2,1)} %bitcast.5), custom_call_target="tpu_custom_call" | custom-call | tf_op jit(solution)/shard_map/pallas_call | solution.py:399
  72.5 0.0 copy-start.1
  72.5 0.0 copy-start
  72.5 3.4 %copy.13 = f32[1,9,8,64,128]{4,3,2,1,0:T(8,128)} copy(f32[1,9,8,64,128]{4,3,2,1,0:T(8,128)} %bitcast.4) | data formatting | bytes 4718592
  75.9 0.0 copy-done.1
  75.9 0.6 copy.14
  76.5 0.0 copy-done
  76.5 0.6 copy.15
Async XLA Ops:
  72.5 3.4 %copy-start.1 = (f32[8,8,128]{2,1,0:T(8,128)S(1)}, f32[8,8,128]{2,1,0:T(8,128)}, u32[]{:S(2)}) copy-start(f32[8,8,128]{2,1,0:T(8,128)} %get-tuple-element.13) | copy-start | bytes 98308
  72.5 4.0 %copy-start = (f32[8,8,128]{2,1,0:T(8,128)S(1)}, f32[8,8,128]{2,1,0:T(8,128)}, u32[]{:S(2)}) copy-start(f32[8,8,128]{2,1,0:T(8,128)} %get-tuple-element.14) | copy-start | bytes 98308
